TPU v7x, 32 devices: a whole 2x2x4 slice. The times are simulated.
32 devices in a mesh: groups: 2 (over x), hist: 8 (over z, y), cand: 2 (over core).
Axes of the slice: x: 2, y: 2, z: 4, core: 2. Of those that a mesh axis runs over, the one named last changes fastest.
Arguments:
- candidates: bfloat16 [16, 1024, 512], P(('groups', 'hist'), 'cand'), parts along dimension 0, may hold values from -6 to 6
- hist_keys: bfloat16 [16, 1024, 512], P('groups', ('hist', 'cand')), parts along dimension 0, may hold values from -10 to 10
- hist_values: bfloat16 [16, 1024, 512], P('groups', ('hist', 'cand')), parts along dimension 0, may hold values from -6 to 6
- block_mask: int32 [16, 8, 8], P(('groups', 'hist')), parts along dimension 0, may hold values 0 or 1
- hist_blocks: int32 [16], P(('groups', 'hist')), parts along dimension 0, may hold values from 1 to 8, as said below
- proj_weight: bfloat16 [512, 1024], replicated, may hold values from -0.25 to 0.25
- out_weight: bfloat16 [512, 512], replicated, may hold values from -0.25 to 0.25
Outputs:
- cand_out: bfloat16 [16, 1024, 512], P(('groups', 'hist'), 'cand'), parts along dimension 0
There are 2 independent parts, one for each index of `groups`. A program takes and returns all parts, laid end to end along the dimension named above; an argument that names none is the same for every part. Nothing has to cross between parts.
Inputs may be any that keep to these rules, and one draw needn't show every extreme that they name: `hist_blocks`: some user has all 8 blocks.
All inputs are finite; a program needn't handle non-finite values. No bound on the sum of `block_mask` on one device may be relied on, other than what follows from the above.
Results may differ from a plain program's by a relative error of at most 0.013.
Values may be sent and summed in bfloat16 or wider, within the bound.
A program may use at most 64 MiB of HBM per device.

v0:
```python
import jax
import jax.numpy as jnp
from jax import lax
from jax.sharding import PartitionSpec as P

HEADS = 8
BLK = 128


EPS = 1e-05


def layer_norm(values_in):
    center = values_in - jnp.mean(values_in, axis=-1, keepdims=True)
    spread = jnp.mean(center * center, axis=-1, keepdims=True)
    return center * lax.rsqrt(spread + EPS)


def attend(running, query_heads, mask_rows, key_piece, value_piece, slab_count, group_rows, stride):
    piece_width = key_piece.shape[1]
    query_count = query_heads.shape[0]
    head_count = query_heads.shape[1]
    head_size = query_heads.shape[2]
    block_count = mask_rows.shape[0]
    block_total = mask_rows.shape[1]
    slab_keys = group_rows * piece_width
    score_scale = head_size ** (-0.5)

    def add_slab(slab_index, summed):
        key_slab = lax.dynamic_slice_in_dim(key_piece, slab_index * group_rows, group_rows, 0)
        value_slab = lax.dynamic_slice_in_dim(value_piece, slab_index * group_rows, group_rows, 0)
        key_slab = key_slab.reshape(slab_keys, head_count, head_size)
        value_slab = value_slab.reshape(slab_keys, head_count, head_size)
        positions = (slab_index * group_rows + jnp.arange(group_rows, dtype=jnp.int32))[
            :, None
        ] * stride
        positions = (positions + jnp.arange(piece_width, dtype=jnp.int32)[None, :]).reshape(
            slab_keys
        )
        onehot = (
            positions[None, :] // BLK == jnp.arange(block_total, dtype=jnp.int32)[:, None]
        ).astype(jnp.float32)
        key_mask = jnp.dot(mask_rows, onehot, preferred_element_type=jnp.float32)
        scores = (
            jnp.einsum("qhd,khd->hqk", query_heads, key_slab, preferred_element_type=jnp.float32)
            * score_scale
        )
        gated_scores = (
            jax.nn.silu(scores).reshape(head_count, block_count, BLK, slab_keys)
            * key_mask[None, :, None, :]
        )
        weights = gated_scores.reshape(head_count, query_count, slab_keys).astype(jnp.bfloat16)
        return summed + jnp.einsum(
            "hqk,khd->qhd", weights, value_slab, preferred_element_type=jnp.float32
        )

    return lax.fori_loop(0, slab_count, add_slab, running)


def on_device(candidates, hist_keys, hist_values, block_mask, hist_blocks, proj_weight, out_weight):
    cand_rows = candidates[0]
    own_count = cand_rows.shape[0]
    width_model = cand_rows.shape[1]
    head_count = HEADS
    head_size = width_model // head_count
    normed = layer_norm(cand_rows.astype(jnp.float32)).astype(jnp.bfloat16)
    projected = jax.nn.silu(
        jnp.dot(normed, proj_weight, preferred_element_type=jnp.float32)
    ).astype(jnp.bfloat16)
    gate_rows = projected[:, :width_model]
    queries = projected[:, width_model:]
    query_heads = queries.reshape(own_count, head_count, head_size)
    block_total = block_mask.shape[2]
    live_blocks = (jnp.arange(block_total, dtype=jnp.int32) < hist_blocks[0]).astype(jnp.float32)
    mask_eff = block_mask[0].astype(jnp.float32) * live_blocks[None, :]
    arrived_keys, arrived_values = (
        lax.all_to_all(hist_keys[:, None], "hist", split_axis=0, concat_axis=1, tiled=True),
        lax.all_to_all(hist_values[:, None], "hist", split_axis=0, concat_axis=1, tiled=True),
    )
    key_rows = arrived_keys[0]
    value_rows = arrived_values[0]
    hist_count = lax.axis_size("hist")
    cand_count = lax.axis_size("cand")
    cand_index = lax.axis_index("cand")
    per_device = key_rows.shape[1]
    stride = cand_count * per_device
    group_rows = min(8, hist_count)
    slab_count = hist_count // group_rows
    own_blocks = own_count // BLK
    own_mask = lax.dynamic_slice_in_dim(mask_eff, cand_index * own_blocks, own_blocks, 0)
    empty = jnp.zeros((own_count, head_count, head_size), jnp.float32)
    attended = attend(
        empty,
        query_heads,
        own_mask,
        lax.all_gather(key_rows, "cand", axis=1, tiled=True),
        lax.all_gather(value_rows, "cand", axis=1, tiled=True),
        slab_count,
        group_rows,
        stride,
    )
    attended = attended.reshape(own_count, width_model)
    mixed = (layer_norm(attended) * gate_rows.astype(jnp.float32)).astype(jnp.bfloat16)
    result = cand_rows.astype(jnp.float32) + jnp.dot(
        mixed, out_weight, preferred_element_type=jnp.float32
    )
    return result.astype(jnp.bfloat16)[None]


def solution(mesh):
    in_specs = (
        P(("groups", "hist"), "cand", None),
        P("groups", ("hist", "cand"), None),
        P("groups", ("hist", "cand"), None),
        P(("groups", "hist"), None, None),
        P(("groups", "hist")),
        P(),
        P(),
    )
    out_specs = P(("groups", "hist"), "cand", None)
    return jax.shard_map(
        on_device, mesh=mesh, in_specs=in_specs, out_specs=out_specs, check_vma=False
    )
```

profile of v0, /device:TPU:0, one launch (start us, length us, event | category | flops | bytes accessed | tf_op | source)
XLA Modules:
  0.0 81.3 jit_solution(10235428924594484104)
XLA Ops:
  6.5 0.0 copy-start
  6.5 0.0 all-gather.5.cloned.1.call-start
  6.5 22.1 %all_to_all.8 = bf16[8,1,64,512]{3,2,1,0:T(8,128)(2,1)} all-to-all(bf16[8,1,64,512]{3,2,1,0:T(8,128)(2,1)} %bitcast.74), channel_id=1, replica_groups=mesh['groups'=2,'hist'=8,'cand'=2] {'hist'}, dimensions={0} | all-to-all | bytes 1048576 | tf_op jit(solution)/shard_map/all_to_all | solution.py:77
  28.6 0.0 all-gather.5.cloned.1.call-update
  28.6 3.6 %all-to-all-start.1 = ((bf16[8,1,64,512]{3,2,1,0:T(8,128)(2,1)}), bf16[8,1,64,512]{3,2,1,0:T(8,128)(2,1)S(1)}, u32[]{:S(2)}, u32[]{:S(2)}) async-start(bf16[8,1,64,512]{3,2,1,0:T(8,128)(2,1)} %bitcast.75), calls=%async_computation.1 | async-start | bytes 1048576 | tf_op jit(solution)/shard_map/all_to_all | solution.py:78
  32.2 0.0 all-gather.7.cloned.1.call-start
  32.3 0.0 copy-done.1
  32.3 0.1 convert_reduce_fusion
  32.5 0.3 fusion.6
  32.8 13.6 %all-to-all-done.1 = bf16[8,1,64,512]{3,2,1,0:T(8,128)(2,1)S(1)} async-done(((bf16[8,1,64,512]{3,2,1,0:T(8,128)(2,1)}), bf16[8,1,64,512]{3,2,1,0:T(8,128)(2,1)S(1)}, u32[]{:S(2)}, u32[]{:S(2)}) %all-to-all-start.1) | async-done | bytes 524320 | tf_op jit(solution)/shard_map/all_to_all | solution.py:78
  46.4 0.8 copy-done.2
  47.2 0.0 all-gather.7.cloned.1.call-update
  47.2 0.0 copy-done
  47.3 1.0 %multiply_convert_fusion.1 = bf16[512,1024]{1,0:T(8,128)(2,1)S(1)} fusion(bf16[512,1024]{1,0:T(8,128)(2,1)S(1)} %copy-done, bf16[1,512,512]{2,1,0:T(8,128)(2,1)S(1)} %copy-done.1, f32[512]{0:T(512)S(1)} %add_rsqrt_fusion.1, f32[512]{0:T(512)S(1)} %broadcast_multiply_fusion.1), kind=kOutput, calls=%fused_computation.1 | convolution fusion | flops 540540928 | bytes 2625536 | tf_op jit(solution)/shard_map/dot_general | solution.py:68
  48.3 0.0 copy-start.3
  48.3 0.0 copy-start.6
  49.1 1.0 %copy.16 = bf16[512,512]{0,1:T(8,128)(2,1)} copy(bf16[512,512]{1,0:T(8,128)(2,1)S(1)} %slice.8) | data formatting | bytes 1048576 | tf_op jit(solution)/shard_map/slice | solution.py:71
  50.1 0.1 add_select_fusion
  50.2 0.0 copy-done.6
  50.2 0.1 fusion.19
  50.3 1.7 %copy.17 = bf16[8,1,128,512]{2,0,3,1:T(8,128)(2,1)S(1)} copy(bf16[8,1,128,512]{3,2,1,0:T(8,128)(2,1)} %all-gather.5.cloned.1.call-done) | data formatting | bytes 2097152 | tf_op jit(solution)/shard_map/all_gather | solution.py:96
  52.0 1.3 %reshape.148 = bf16[1024,8,64]{0,2,1:T(8,128)(2,1)} reshape(bf16[8,1,128,512]{2,0,3,1:T(8,128)(2,1)S(1)} %copy.17) | data formatting | bytes 2097152 | tf_op jit(solution)/shard_map/while/body/eval_jaxpr/reshape | solution.py:32
  53.3 2.2 %all-gather.7.cloned.1.call-done = bf16[8,1,128,512]{3,2,1,0:T(8,128)(2,1)} async-done(((bf16[8,1,64,512]{3,2,1,0:T(8,128)(2,1)}), bf16[8,1,128,512]{3,2,1,0:T(8,128)(2,1)}) %all-gather.7.cloned.1.call-update) | async-done | bytes 1048592 | tf_op jit(solution)/shard_map/all_gather | solution.py:97
  55.5 1.7 %copy.18 = bf16[8,1,128,512]{2,0,3,1:T(8,128)(2,1)S(1)} copy(bf16[8,1,128,512]{3,2,1,0:T(8,128)(2,1)} %all-gather.7.cloned.1.call-done) | data formatting | bytes 2097152 | tf_op jit(solution)/shard_map/all_gather | solution.py:97
  57.2 1.3 %reshape.149 = bf16[1024,8,64]{0,2,1:T(8,128)(2,1)} reshape(bf16[8,1,128,512]{2,0,3,1:T(8,128)(2,1)S(1)} %copy.18) | data formatting | bytes 2097152 | tf_op jit(solution)/shard_map/while/body/eval_jaxpr/reshape | solution.py:33
  58.5 1.6 %mul.90 = f32[4,128,1024]{2,1,0:T(8,128)} broadcast(f32[4,1024]{1,0:T(4,128)S(1)} %fusion.19), dimensions={0,2} | broadcast | bytes 2113536 | tf_op jit(solution)/shard_map/while/body/eval_jaxpr/mul | solution.py:49
  60.1 10.2 %fusion.28 = (f32[512]{0:T(512)S(1)}, f32[8,512,64]{1,2,0:T(8,128)S(1)}) fusion(bf16[1024,8,64]{0,2,1:T(8,128)(2,1)} %reshape.149, bf16[512,8,64]{0,2,1:T(8,128)(2,1)S(1)} %bitcast.76, bf16[1024,8,64]{0,2,1:T(8,128)(2,1)} %reshape.148, f32[512,1024]{1,0:T(8,128)} %bitcast.73), kind=kOutput, calls=%fused_computation.47 | convolution fusion | flops 1103363584 | bytes 5769216 | tf_op jit(solution)/shard_map/while/body/eval_jaxpr/hqk,khd->qhd/dot_general | solution.py:53
  70.3 0.0 copy-start.5
  70.3 0.2 fusion.9
  70.5 1.3 %copy.19 = f32[512,512]{1,0:T(8,128)} copy(f32[512,512]{0,1:T(8,128)S(1)} %bitcast.72) | data formatting | bytes 2097152 | tf_op jit(solution)/shard_map/reshape | solution.py:102
  71.8 0.0 copy-done.5
  71.8 2.7 %fusion.5 = bf16[1,512,512]{2,1,0:T(8,128)(2,1)} fusion(bf16[512,512]{1,0:T(8,128)(2,1)S(1)} %copy-done.5, bf16[1,512,512]{2,1,0:T(8,128)(2,1)S(1)} %copy-done.1, f32[512,512]{1,0:T(8,128)} %copy.19, bf16[512,1024]{1,0:T(8,128)(2,1)} %copy-done.3, f32[512]{0:T(512)S(1)} %add_rsqrt_fusion, f32[512]{0:T(512)S(1)} %broadcast_multiply_fusion), kind=kOutput, calls=%fused_computation.10 | convolution fusion | flops 270532608 | bytes 3149824 | tf_op jit(solution)/shard_map/dot_general | solution.py:104
  (14 shorter events, 0.1 us)
Async XLA Ops:
  6.5 40.7 %copy-start = (bf16[512,1024]{1,0:T(8,128)(2,1)S(1)}, bf16[512,1024]{1,0:T(8,128)(2,1)}, u32[]{:S(2)}) copy-start(bf16[512,1024]{1,0:T(8,128)(2,1)} %param.12) | copy-start | bytes 3145732
  6.5 25.8 %copy-start.1 = (bf16[1,512,512]{2,1,0:T(8,128)(2,1)S(1)}, bf16[1,512,512]{2,1,0:T(8,128)(2,1)}, u32[]{:S(2)}) copy-start(bf16[1,512,512]{2,1,0:T(8,128)(2,1)} %param.7) | copy-start | bytes 1572868
  6.5 43.8 %all-gather.5.cloned.1.call-start = ((), (), s32[]{:S(2)}) async-start(), calls=%async_computation.2 | async-start | bytes 1572864 | tf_op jit(solution)/shard_map/all_gather | solution.py:96
  28.6 17.8 %all-to-all-start.1 = ((bf16[8,1,64,512]{3,2,1,0:T(8,128)(2,1)}), bf16[8,1,64,512]{3,2,1,0:T(8,128)(2,1)S(1)}, u32[]{:S(2)}, u32[]{:S(2)}) async-start(bf16[8,1,64,512]{3,2,1,0:T(8,128)(2,1)} %bitcast.75), calls=%async_computation.1 | async-start | bytes 1048576 | tf_op jit(solution)/shard_map/all_to_all | solution.py:78
  32.2 23.2 %all-gather.7.cloned.1.call-start = ((), (), s32[]{:S(2)}) async-start(), calls=%async_computation.3 | async-start | bytes 1572864 | tf_op jit(solution)/shard_map/all_gather | solution.py:97
  46.4 0.8 copy-start.2
  48.3 2.0 %copy-start.3 = (bf16[512,1024]{1,0:T(8,128)(2,1)}, bf16[512,1024]{1,0:T(8,128)(2,1)S(1)}, u32[]{:S(2)}) copy-start(bf16[512,1024]{1,0:T(8,128)(2,1)S(1)} %multiply_convert_fusion.1) | copy-start | bytes 3145732
  48.3 1.9 %copy-start.6 = (s32[1,8,8]{2,1,0:T(8,128)S(1)}, s32[1,8,8]{2,1,0:T(8,128)}, u32[]{:S(2)}) copy-start(s32[1,8,8]{2,1,0:T(8,128)} %param.10) | copy-start | bytes 772
  57.2 2.9 %copy-start.4 = (bf16[512,512]{0,1:T(8,128)(2,1)S(1)}, bf16[512,512]{0,1:T(8,128)(2,1)}, u32[]{:S(2)}) copy-start(bf16[512,512]{0,1:T(8,128)(2,1)} %copy.16) | copy-start | bytes 1572868
  70.3 1.5 %copy-start.5 = (bf16[512,512]{1,0:T(8,128)(2,1)S(1)}, bf16[512,512]{1,0:T(8,128)(2,1)}, u32[]{:S(2)}) copy-start(bf16[512,512]{1,0:T(8,128)(2,1)} %param.13) | copy-start | bytes 1572868
Sparse Core Ops, SparseCore 0:
  28.8 8.0 all-gather.4
  47.4 8.0 all-gather.6
where the time goes:
time: 81.7 us; the launch traced here: 81.3 us
  blocking collectives  22.1 us (27%)
  waiting for transfers between devices  15.8 us (19%)
  between operations  14.2 us (17%)
  matrix products  14 us (17%)
  local copies, waits for them, and re-layouts  10.8 us (13%)
  starting transfers between devices  3.64 us (4%)
    all_to_all x1, blocking collectives, on_device(): lax.all_to_all(hist_keys[:, None], 'hist', split_axis=0, concat_axis=1, t...  22.1 us
    all_to_all x1, waiting for transfers between devices, on_device(): lax.all_to_all(hist_values[:, None], 'hist', split_axis=0, concat_axis=1,...  13.6 us
    dot_general x1, matrix products, add_slab(): jnp.einsum('hqk,khd->qhd', weights, value_slab, preferred_element_type=jn...  10.2 us
    all_to_all x1, starting transfers between devices, on_device(): lax.all_to_all(hist_values[:, None], 'hist', split_axis=0, concat_axis=1,...  3.61 us
    dot_general x1, matrix products, on_device(): jnp.dot(mixed, out_weight, preferred_element_type=jnp.float32)  2.66 us
    all_gather x1, waiting for transfers between devices, on_device(): lax.all_gather(value_rows, 'cand', axis=1, tiled=True)  2.16 us
    all_gather x1, local copies, waits for them, and re-layouts, on_device(): lax.all_gather(key_rows, 'cand', axis=1, tiled=True)  1.72 us
    all_gather x1, local copies, waits for them, and re-layouts, on_device(): lax.all_gather(value_rows, 'cand', axis=1, tiled=True)  1.71 us
  transfers between devices with their start and end apart: 3, of which 2 were waited for; matrix products, arithmetic and copies ran while one was open for 7% of the time, Pallas kernels for 0%

commit v1 on v0

v1 whole, which is shorter than its diff:
```python
import functools

import jax
import jax.numpy as jnp
from jax import lax
from jax.experimental import pallas as pl
from jax.experimental.pallas import tpu as pltpu
from jax.sharding import PartitionSpec as P

HEADS = 8
BLK = 128
GROUP = 4
EPS = 1e-05
MESH = pl.DeviceIdType.MESH


def layer_norm(values_in):
    center = values_in - jnp.mean(values_in, axis=-1, keepdims=True)
    spread = jnp.mean(center * center, axis=-1, keepdims=True)
    return center * lax.rsqrt(spread + EPS)


def silu(values_in):
    half = values_in * 0.5
    return half + half * jnp.tanh(half)


def partner_of(me, step, count):
    if count & (count - 1) == 0:
        other = 0
        bit = 1
        while bit < count:
            other = other + ((me // bit + step // bit) % 2) * bit
            bit *= 2
        return other, other
    return (me + count - step) % count, (me + step) % count


def spread_heads(piece, head_size):
    width = piece.shape[1]
    lanes = lax.broadcasted_iota(jnp.int32, piece.shape, 1) // head_size
    zero = jnp.zeros_like(piece)
    return jnp.concatenate(
        [jnp.where(lanes == head, piece, zero) for head in range(width // head_size)], axis=0
    )


def kernel(
    hist_count, cand_count,
    mask_ref, len_ref, cand_hbm, keys_hbm, values_hbm, proj_hbm, outw_hbm,
    out_ref,
    cand_v, proj_v, outw_v, key_buf, value_buf, query_v, gate_v, total_v, masked_v,
    in_sem, own_sem, send_sem, recv_sem, fsend_sem, frecv_sem,
):
    me = lax.axis_index("hist")
    core = lax.axis_index("cand")
    own_rows, width = cand_v.shape
    head_size = width // HEADS
    group_width = GROUP * head_size
    own_blocks = own_rows // BLK
    scale = 0.5 * head_size ** (-0.5)

    cand_in = pltpu.make_async_copy(cand_hbm.at[0], cand_v, in_sem.at[0])
    proj_in = pltpu.make_async_copy(proj_hbm, proj_v, in_sem.at[1])
    outw_in = pltpu.make_async_copy(outw_hbm, outw_v, in_sem.at[2])
    cand_in.start()
    proj_in.start()
    outw_in.start()
    own_in = [
        pltpu.make_async_copy(src.at[me], buf.at[0, core], own_sem.at[i])
        for i, (src, buf) in enumerate(((keys_hbm, key_buf), (values_hbm, value_buf)))
    ]
    for copy in own_in:
        copy.start()

    barrier = pltpu.get_barrier_semaphore()
    for step in range(1, hist_count):
        _, dst = partner_of(me, step, hist_count)
        pl.semaphore_signal(barrier, inc=1, device_id={"hist": dst}, device_id_type=MESH)
    for turn in range(1, cand_count):
        pl.semaphore_signal(
            barrier, inc=1, device_id={"cand": (core + turn) % cand_count}, device_id_type=MESH
        )
    pl.semaphore_wait(barrier, hist_count - 1 + cand_count - 1)

    def direct(step, kind):
        _, dst = partner_of(me, step, hist_count)
        src, buf = ((keys_hbm, key_buf), (values_hbm, value_buf))[kind]
        return pltpu.make_async_remote_copy(
            src_ref=src.at[dst],
            dst_ref=buf.at[step, core],
            send_sem=send_sem.at[step, kind],
            recv_sem=recv_sem.at[step, kind],
            device_id={"hist": dst},
            device_id_type=MESH,
        )

    def forward(step, kind, turn, first=False):
        src, buf = ((keys_hbm, key_buf), (values_hbm, value_buf))[kind]
        return pltpu.make_async_remote_copy(
            src_ref=src.at[me] if first else buf.at[step, core],
            dst_ref=buf.at[step, core],
            send_sem=fsend_sem.at[step, turn - 1, kind],
            recv_sem=frecv_sem.at[step, turn - 1, kind],
            device_id={"cand": (core + turn) % cand_count},
            device_id_type=MESH,
        )

    for step in range(1, hist_count):
        for kind in range(2):
            direct(step, kind).start()
    for turn in range(1, cand_count):
        for kind in range(2):
            forward(0, kind, turn, True).start()

    cand_in.wait()
    proj_in.wait()
    normed = layer_norm(cand_v[...].astype(jnp.float32)).astype(jnp.bfloat16)
    gate_v[...] = silu(
        jnp.dot(normed, proj_v[:, :width], preferred_element_type=jnp.float32)
    ).astype(jnp.bfloat16)
    query_v[...] = silu(
        jnp.dot(normed, proj_v[:, width:], preferred_element_type=jnp.float32)
    ).astype(jnp.bfloat16)
    total_v[...] = jnp.zeros_like(total_v)

    def mask_queries(step):
        source, _ = partner_of(me, step, hist_count)
        live = jnp.clip(len_ref[0] - source, 0, 1)
        for block in range(own_blocks):
            factor = (mask_ref[0, core * own_blocks + block, source] * live).astype(
                jnp.float32
            ) * scale
            rows = pl.ds(block * BLK, BLK)
            masked_v[rows, :] = (query_v[rows, :].astype(jnp.float32) * factor).astype(jnp.bfloat16)

    def attend(step, owner):
        for group in range(width // group_width):
            columns = pl.ds(group * group_width, group_width)
            keys = spread_heads(key_buf[step, owner, :, columns], head_size)
            values = spread_heads(value_buf[step, owner, :, columns], head_size)
            half = lax.dot_general(
                masked_v[:, columns], keys, (((1,), (1,)), ((), ())),
                preferred_element_type=jnp.float32,
            )
            weights = (half + half * jnp.tanh(half)).astype(jnp.bfloat16)
            total_v[:, columns] += jnp.dot(weights, values, preferred_element_type=jnp.float32)

    def others(step):
        for turn in range(1, cand_count):
            for kind in range(2):
                forward(step, kind, turn).wait_recv()
            attend(step, (core + cand_count - turn) % cand_count)

    mask_queries(0)
    for copy in own_in:
        copy.wait()
    attend(0, core)
    others(0)

    def one_step(step, carry):
        mask_queries(step)
        for kind in range(2):
            direct(step, kind).wait_recv()
            for turn in range(1, cand_count):
                forward(step, kind, turn).start()
        attend(step, core)
        others(step)
        return carry

    lax.fori_loop(1, hist_count, one_step, 0)

    outw_in.wait()
    mixed = (layer_norm(total_v[...]) * gate_v[...].astype(jnp.float32)).astype(jnp.bfloat16)
    result = cand_v[...].astype(jnp.float32) + jnp.dot(
        mixed, outw_v[...], preferred_element_type=jnp.float32
    )
    out_ref[0] = result.astype(jnp.bfloat16)

    for turn in range(1, cand_count):
        for kind in range(2):
            forward(0, kind, turn, True).wait_send()

    def drain(step, carry):
        for kind in range(2):
            direct(step, kind).wait_send()
            for turn in range(1, cand_count):
                forward(step, kind, turn).wait_send()
        return carry

    lax.fori_loop(1, hist_count, drain, 0)


def on_device(candidates, hist_keys, hist_values, block_mask, hist_blocks, proj_weight, out_weight):
    hist_count = lax.axis_size("hist")
    cand_count = lax.axis_size("cand")
    _, own_rows, width = candidates.shape
    piece = hist_keys.shape[1]
    anywhere = pl.BlockSpec(memory_space=pl.ANY)
    scalars = pl.BlockSpec(memory_space=pltpu.SMEM)
    bf16 = jnp.bfloat16
    return pl.pallas_call(
        functools.partial(kernel, hist_count, cand_count),
        out_shape=jax.ShapeDtypeStruct(candidates.shape, bf16),
        in_specs=[scalars, scalars] + [anywhere] * 5,
        out_specs=pl.BlockSpec(memory_space=pltpu.VMEM),
        scratch_shapes=[
            pltpu.VMEM((own_rows, width), bf16),
            pltpu.VMEM(proj_weight.shape, bf16),
            pltpu.VMEM(out_weight.shape, bf16),
            pltpu.VMEM((hist_count, cand_count, piece, width), bf16),
            pltpu.VMEM((hist_count, cand_count, piece, width), bf16),
            pltpu.VMEM((own_rows, width), bf16),
            pltpu.VMEM((own_rows, width), bf16),
            pltpu.VMEM((own_rows, width), jnp.float32),
            pltpu.VMEM((own_rows, width), bf16),
            pltpu.SemaphoreType.DMA((3,)),
            pltpu.SemaphoreType.DMA((2,)),
            pltpu.SemaphoreType.DMA((hist_count, 2)),
            pltpu.SemaphoreType.DMA((hist_count, 2)),
            pltpu.SemaphoreType.DMA((hist_count, max(cand_count - 1, 1), 2)),
            pltpu.SemaphoreType.DMA((hist_count, max(cand_count - 1, 1), 2)),
        ],
        compiler_params=pltpu.CompilerParams(collective_id=0, has_side_effects=True),
    )(block_mask, hist_blocks, candidates, hist_keys, hist_values, proj_weight, out_weight)


def solution(mesh):
    in_specs = (
        P(("groups", "hist"), "cand", None),
        P("groups", ("hist", "cand"), None),
        P("groups", ("hist", "cand"), None),
        P(("groups", "hist"), None, None),
        P(("groups", "hist")),
        P(),
        P(),
    )
    out_specs = P(("groups", "hist"), "cand", None)
    return jax.shard_map(
        on_device, mesh=mesh, in_specs=in_specs, out_specs=out_specs, check_vma=False
    )
```

time: 81.7 us -> 35.9 us (0.44)
  Pallas kernels: 0 us -> 33 us
  blocking collectives: 22.1 us -> 0 us
  waiting for transfers between devices: 15.8 us -> 0 us
  matrix products: 14 us -> 0 us
  between operations: 14.2 us -> 0.66 us
  local copies, waits for them, and re-layouts: 10.8 us -> 1.87 us
  starting transfers between devices: 3.64 us -> 0 us
    pallas_call x0 -> x1, Pallas kernels: none -> 33 us  [on_device(): pl.pallas_call(functools.partial(kernel, hist_count, cand_count), out_sha...]
    all_to_all x1 -> x0, blocking collectives: 22.1 us -> none  [on_device(): lax.all_to_all(hist_keys[:, None], 'hist', split_axis=0, concat_axis=1, t...]
    dot_general x4 -> x0, matrix products: 14 us -> none  [the longest x1 10.2 us: add_slab(): jnp.einsum('hqk,khd->qhd', weights, value_slab, preferred_element_type=jn...]
    all_to_all x1 -> x0, waiting for transfers between devices: 13.6 us -> none  [on_device(): lax.all_to_all(hist_values[:, None], 'hist', split_axis=0, concat_axis=1,...]
    reshape x3 -> x0, local copies, waits for them, and re-layouts: 3.87 us -> none  [the longest x1 1.31 us: on_device(): attended = attended.reshape(own_count, width_model)]
    all_to_all x1 -> x0, starting transfers between devices: 3.61 us -> none  [on_device(): lax.all_to_all(hist_values[:, None], 'hist', split_axis=0, concat_axis=1,...]
    all_gather x2 -> x0, local copies, waits for them, and re-layouts: 3.43 us -> none  [the longest x1 1.72 us: on_device(): lax.all_gather(key_rows, 'cand', axis=1, tiled=True)]
    all_gather x2 -> x0, waiting for transfers between devices: 2.16 us -> none  [the longest x1 2.16 us: on_device(): lax.all_gather(value_rows, 'cand', axis=1, tiled=True)]
  transfers between devices with their start and end apart: 3 -> 0, of which waited for: 2 -> 0; matrix products, arithmetic and copies ran while one was open for 7% -> 0% of each run, Pallas kernels for 0% -> 0%
where the time goes in v1:
time: 35.9 us; the launch traced here: 35.6 us
  Pallas kernels  33 us (92%)
  local copies, waits for them, and re-layouts  1.87 us (5%)
  between operations  0.66 us (2%)
    pallas_call x1, Pallas kernels, on_device(): pl.pallas_call(functools.partial(kernel, hist_count, cand_count), out_sha...  33 us
    unnamed x1, local copies, waits for them, and re-layouts  1.87 us

profile of v1, /device:TPU:0, one launch (start us, length us, event | category | flops | bytes accessed | tf_op | source)
XLA Modules:
  0.0 35.6 jit_solution(16384972189374069688)
XLA Ops:
  0.7 33.0 %shard_map.73 = bf16[1,512,512]{2,1,0:T(8,128)(2,1)} custom-call(s32[1,8,8]{2,1,0:T(8,128)} %mask_ref.1, s32[1]{0:T(128)S(6)} %copy.9.len_ref, bf16[1,512,512]{2,1,0:T(8,128)(2,1)} %cand_hbm.1, bf16[8,64,512]{2,1,0:T(8,128)(2,1)} %keys_hbm.1, bf16[8,64,512]{2,1,0:T(8,128)(2,1)} %values_hbm.1, bf16[512,1024]{1,0:T(8,128)(2,1)} %proj_hbm.1, ...), custom_call_target="tpu_custom_call" | custom-call | tf_op jit(solution)/shard_map/pallas_call | solution.py:202
  33.7 1.9 %copy.10 = bf16[1,512,512]{2,1,0:T(8,128)(2,1)} copy(bf16[1,512,512]{2,1,0:T(8,128)(2,1)} %shard_map.73) | data formatting | bytes 1048576

commit v2 on v1

--- a/solution.py
+++ b/solution.py
@@ -10,6 +10,7 @@
 HEADS = 8
 BLK = 128
 GROUP = 4
+UNROLLED = 8
 EPS = 1e-05
 MESH = pl.DeviceIdType.MESH
 
@@ -34,6 +35,17 @@
             bit *= 2
         return other, other
     return (me + count - step) % count, (me + step) % count
+
+
+def step_order(count):
+    if count & (count - 1) or count < 4:
+        return list(range(1, count))
+    bits = (count // 2).bit_length() - 1
+    order = []
+    for pair in range(count // 2):
+        turned = sum((pair >> bit & 1) << (bits - 1 - bit) for bit in range(bits))
+        order += [turned * 2, turned * 2 + 1]
+    return order[1:]
 
 
 def spread_heads(piece, head_size):
@@ -106,7 +118,8 @@
             device_id_type=MESH,
         )
 
-    for step in range(1, hist_count):
+    order = step_order(hist_count)
+    for step in order:
         for kind in range(2):
             direct(step, kind).start()
     for turn in range(1, cand_count):
@@ -168,7 +181,11 @@
         others(step)
         return carry
 
-    lax.fori_loop(1, hist_count, one_step, 0)
+    if hist_count <= UNROLLED:
+        for step in order:
+            one_step(step, 0)
+    else:
+        lax.fori_loop(1, hist_count, one_step, 0)
 
     outw_in.wait()
     mixed = (layer_norm(total_v[...]) * gate_v[...].astype(jnp.float32)).astype(jnp.bfloat16)
@@ -201,7 +218,7 @@
     bf16 = jnp.bfloat16
     return pl.pallas_call(
         functools.partial(kernel, hist_count, cand_count),
-        out_shape=jax.ShapeDtypeStruct(candidates.shape, bf16),
+        out_shape=pltpu.VMEM(candidates.shape, bf16),
         in_specs=[scalars, scalars] + [anywhere] * 5,
         out_specs=pl.BlockSpec(memory_space=pltpu.VMEM),
         scratch_shapes=[

time: 35.9 us -> 33 us (0.919)
  the two profiles are of different devices: /device:TPU:0 before, /device:TPU:11 now
where the time goes in v2:
time: 33 us; the launch traced here: 32.8 us
  Pallas kernels  31.4 us (95%)
  local copies, waits for them, and re-layouts  0.8 us (2%)
  between operations  0.66 us (2%)
    pallas_call x1, Pallas kernels, on_device(): pl.pallas_call(functools.partial(kernel, hist_count, cand_count), out_sha...  31.4 us
    unnamed x1, local copies, waits for them, and re-layouts  0.8 us

profile of v2, /device:TPU:11, one launch (start us, length us, event | category | flops | bytes accessed | tf_op | source)
XLA Modules:
  0.0 32.8 jit_solution(3436365576411702000)
XLA Ops:
  0.7 31.4 %shard_map.73 = bf16[1,512,512]{2,1,0:T(8,128)(2,1)S(1)} custom-call(s32[1,8,8]{2,1,0:T(8,128)} %mask_ref.1, s32[1]{0:T(128)S(6)} %copy.10.len_ref, bf16[1,512,512]{2,1,0:T(8,128)(2,1)} %cand_hbm.1, bf16[8,64,512]{2,1,0:T(8,128)(2,1)} %keys_hbm.1, bf16[8,64,512]{2,1,0:T(8,128)(2,1)} %values_hbm.1, bf16[512,1024]{1,0:T(8,128)(2,1)} %proj_hbm.1, ...), custom_call_target="tpu_custom_call" | custom-call | tf_op jit(solution)/shard_map/pallas_call | solution.py:219
  32.0 0.8 %copy.9 = bf16[1,512,512]{2,1,0:T(8,128)(2,1)} copy(bf16[1,512,512]{2,1,0:T(8,128)(2,1)S(1)} %shard_map.73) | data formatting | bytes 1048576
